TPU v7x, 32 devices: a whole 2x2x4 slice. The times are simulated.
32 devices in a mesh: tm: 8 (over y, x, core), space: 4 (over z).
Axes of the slice: x: 2, y: 2, z: 4, core: 2. Of those that a mesh axis runs over, the one named last changes fastest.
Arguments:
- node_fields: float32 [8, 5, 32, 128, 128], P('tm', None, 'space'), may hold values from -6 to 6
- region_label: int32 [32, 128, 128], P('space'), may hold values from 0 to 3
- sheet_shift: int32 [8, 128], P('tm'), may hold values from 0 to 1
- diffusivity: float32 [4], replicated, may hold values from 0.02 to 0.15
Outputs:
- updated_nodes: float32 [8, 5, 32, 128, 128], P('tm', None, 'space')
All inputs are finite; a program needn't handle non-finite values.
Results may differ from a plain program's by a relative error of at most 0.00002.
Values sent between devices are 32-bit elements; how exact they have to be, the bound alone decides.
A program may use at most 64 MiB of HBM per device.

v0:
```python
import math

import jax
import jax.numpy as jnp
import numpy as np
from jax import lax
from jax.experimental import pallas as pl
from jax.experimental.pallas import tpu as pltpu
from jax.sharding import PartitionSpec as P

NODES = 5
FINE_SWEEPS = 2
BLOCK_Z = 4
BLOCK_X = 2
PAD = 8
PIECES = 4
MESH = pl.DeviceIdType.MESH

slice_length = 1.0


def node_tables():
    radius = math.sqrt(3.0 / 7.0)
    points = [0.0, (1.0 - radius) / 2.0, 0.5, (1.0 + radius) / 2.0, 1.0]
    integrals = np.zeros((4, 5))
    for column in range(5):
        coeffs = [1.0]
        divisor = 1.0
        for other in range(5):
            if other != column:
                anchor = points[other]
                product = [0.0] * (len(coeffs) + 1)
                for degree in range(len(coeffs)):
                    product[degree + 1] = product[degree + 1] + coeffs[degree]
                    product[degree] = product[degree] - anchor * coeffs[degree]
                coeffs = product
                divisor = divisor * (points[column] - anchor)
        for row in range(4):
            bottom = points[row]
            summit = points[row + 1]
            amount = 0.0
            for degree in range(len(coeffs)):
                amount = amount + coeffs[degree] / (degree + 1) * (
                    summit ** (degree + 1) - bottom ** (degree + 1)
                )
            integrals[row, column] = amount / divisor
    return (np.array(points), integrals)


TIMES, INTEGRALS = node_tables()
WEIGHTS = INTEGRALS.sum(axis=0)
STEPS = NODES - 1
EXCHANGES = 2 + FINE_SWEEPS * STEPS


class Transfer:
    def __init__(self, src, dst, send_sem, recv_sem, device, sends, receives):
        self.copy = pltpu.make_async_remote_copy(
            src_ref=src,
            dst_ref=dst,
            send_sem=send_sem,
            recv_sem=recv_sem,
            device_id=device,
            device_id_type=MESH,
        )
        self.sends, self.receives = sends, receives

    def start(self):
        pl.when(self.sends)(self.copy.start)

    def wait_recv(self):
        pl.when(self.receives)(self.copy.wait_recv)

    def wait_send(self):
        pl.when(self.sends)(self.copy.wait_send)


def kernel(
    fields_in, label_in, shift_in, table_in, out, fields, label, shift, table,
    kappa, kappa_c, start, moved, shift_next, below, pads, values, mids, spread, gain, lift, delta, ahead, fold,
    halo_send, halo_recv, time_send, time_recv, load_sem,
):
    n, s = lax.axis_index("tm"), lax.axis_index("space")
    slices, slabs = lax.axis_size("tm"), lax.axis_size("space")
    depth, width, height = label.shape
    rows_c = width // BLOCK_X
    depth_c = depth // BLOCK_Z
    chunk = min(64, width)
    piece = width // PIECES
    last = NODES - 1
    has_prev, has_next = n > 0, n < slices - 1
    has_low, has_high = s > 0, s < slabs - 1
    inner = pl.ds(PAD, width)

    loads = [
        pltpu.make_async_copy(fields_in.at[node], fields.at[node], load_sem.at[node])
        for node in range(NODES)
    ]
    loads += [
        pltpu.make_async_copy(label_in, label, load_sem.at[NODES]),
        pltpu.make_async_copy(shift_in, shift, load_sem.at[NODES + 1]),
        pltpu.make_async_copy(table_in, table, load_sem.at[NODES + 2]),
    ]
    for load in loads:
        load.start()

    barrier = pltpu.get_barrier_semaphore()
    met = jnp.int32(0)
    for dn in (-1, 0, 1):
        for ds in (-1, 0, 1):
            if dn == 0 and ds == 0:
                continue
            there = (n + dn >= 0) & (n + dn < slices) & (s + ds >= 0) & (s + ds < slabs)

            @pl.when(there)
            def _(dn=dn, ds=ds):
                pl.semaphore_signal(
                    barrier, inc=1, device_id={"tm": n + dn, "space": s + ds}, device_id_type=MESH
                )

            met = met + there.astype(jnp.int32)
    pl.semaphore_wait(barrier, met)

    shipped = []

    def send(transfer):
        transfer.start()
        shipped.append(transfer)
        return transfer

    def halo(index, source=None):
        buf = pads.at[index]
        pieces = []
        for k in range(PIECES):
            rows = pl.ds(PAD + k * piece, piece)
            if source is None:
                low, high = buf.at[1, rows], buf.at[depth, rows]
            else:
                low, high = (source.at[z, pl.ds(k * piece, piece)] for z in (0, depth - 1))
            sem = 2 * (index * PIECES + k)
            up = Transfer(
                high, buf.at[0, rows], halo_send.at[sem], halo_recv.at[sem],
                {"space": s + 1}, has_high, has_low,
            )
            down = Transfer(
                low, buf.at[depth + 1, rows], halo_send.at[sem + 1], halo_recv.at[sem + 1],
                {"space": s - 1}, has_low, has_high,
            )
            pieces.append((down, up))
        return pieces

    def arrive(pieces):
        for down, up in pieces:
            down.wait_recv()
            up.wait_recv()

    def time_hop(index, src, dst, ds=0):
        to = {"tm": n + 1} if ds == 0 else {"tm": n + 1, "space": s + ds}
        goes = has_next if ds == 0 else has_next & (s + ds >= 0) & (s + ds < slabs)
        comes = has_prev if ds == 0 else has_prev & (s - ds >= 0) & (s - ds < slabs)
        return Transfer(src, dst, time_send.at[index], time_recv.at[index], to, goes, comes)

    shift_hop = Transfer(
        shift_in, shift_next, time_send.at[0], time_recv.at[0], {"tm": n - 1}, has_prev, has_next
    )
    send(shift_hop)
    end_halo = halo(1, fields_in.at[last])
    for down, up in end_halo:
        send(down)
        send(up)
    start_hop = send(time_hop(1, fields_in.at[last], start))

    first_slice = (n == 0).astype(jnp.float32)

    def sideways(center):
        lane = lax.broadcasted_iota(jnp.int32, center.shape, 1)
        return jnp.where(lane == height - 1, 0.0, pltpu.roll(center, height - 1, 1)) + jnp.where(
            lane == 0, 0.0, pltpu.roll(center, 1, 1)
        )

    def rate(index, z, r, advect, chunk=chunk):
        center = pads[index, z + 1, pl.ds(PAD + r, chunk)]
        behind = pads[index, z + 1, pl.ds(PAD - 1 + r, chunk)]
        total = pads[index, z, pl.ds(PAD + r, chunk)] + pads[index, z + 2, pl.ds(PAD + r, chunk)]
        total = total + (behind + pads[index, z + 1, pl.ds(PAD + 1 + r, chunk)])
        total = total + sideways(center) - 6.0 * center
        return kappa[z, pl.ds(r, chunk)] * total - advect * (center - behind)

    def fill(index, z, r, value):
        rows = value.shape[0]
        pads[index, z + 1, pl.ds(PAD + r, rows)] = value
        if r == 0:
            pads[index, z + 1, pl.ds(PAD + width, 1)] = value[:1]
        if r + rows == width:
            pads[index, z + 1, pl.ds(PAD - 1, 1)] = value[rows - 1 :]

    def each(lo, hi, body):
        def turn(z, carry):
            for r in range(0, width, chunk):
                body(z, r, chunk)
            return carry

        lax.fori_loop(lo, hi, turn, 0)

    def edges(body, needs=None, gives=None):
        for k in range(PIECES):
            if needs is not None:
                arrive(needs[k : k + 1])
            body(0, k * piece, piece)
            body(depth - 1, k * piece, piece)
            if gives is not None:
                send(gives[k][0])
                send(gives[k][1])

    def interior(body):
        each(1, depth - 1, body)

    def weigh(z, r, chunk):
        at = pl.ds(r, chunk)
        total = (first_slice * float(WEIGHTS[0])) * fields[0, z, at]
        for node in range(1, NODES):
            total = total + float(WEIGHTS[node]) * fields[node, z, at]
        fill(0, z, r, total)

    for load in loads:
        load.wait()
    weighted_halo = halo(0)
    edges(weigh, None, weighted_halo)
    interior(weigh)

    def prepare(z, r, chunk):
        at = pl.ds(r, chunk)
        fill(1, z, r, fields[last, z, at])
        labels = label[z, at]
        total = jnp.zeros((chunk, height), jnp.float32)
        for region in range(table.shape[0]):
            total = total + jnp.where(labels == region, table[region], 0.0)
        kappa[z, at] = total

    each(0, depth, prepare)

    for index in range(EXCHANGES):

        @pl.when(jnp.logical_not(has_low))
        def _(index=index):
            pads[index, 0, inner] = jnp.zeros((width, height), jnp.float32)

        @pl.when(jnp.logical_not(has_high))
        def _(index=index):
            pads[index, depth + 1, inner] = jnp.zeros((width, height), jnp.float32)

    def restrict(target, layer_of):
        def turn(zc, carry):
            for r in range(0, width, chunk):
                total = layer_of(BLOCK_Z * zc, r)
                for k in range(1, BLOCK_Z):
                    total = total + layer_of(BLOCK_Z * zc + k, r)
                fold[pl.ds(r, chunk)] = total
            total = fold[pl.ds(0, rows_c, stride=BLOCK_X)]
            for k in range(1, BLOCK_X):
                total = total + fold[pl.ds(k, rows_c, stride=BLOCK_X)]
            target[zc] = total * (1.0 / (BLOCK_Z * BLOCK_X))
            return carry

        lax.fori_loop(0, depth_c, turn, 0)

    advect = shift[...].astype(jnp.float32) / slice_length

    shift_hop.wait_recv()
    arrive(end_halo)
    advect_next = shift_next[...].astype(jnp.float32) / slice_length
    restrict(
        lift,
        lambda z, r: fields[last, z, pl.ds(r, chunk)]
        + (slice_length * float(WEIGHTS[0])) * rate(1, z, r, advect_next),
    )
    lift_hop = send(time_hop(2, lift, moved))

    restrict(kappa_c, lambda z, r: kappa[z, pl.ds(r, chunk)])
    arrive(weighted_halo)
    restrict(
        gain,
        lambda z, r: first_slice * fields[0, z, pl.ds(r, chunk)]
        - fields[last, z, pl.ds(r, chunk)]
        + slice_length * rate(0, z, r, advect),
    )

    @pl.when(jnp.logical_not(has_prev))
    def _():
        moved[...] = jnp.zeros_like(moved)
        delta[...] = jnp.zeros_like(delta)
        below[...] = jnp.zeros_like(below)

    @pl.when(has_prev & jnp.logical_not(has_low))
    def _():
        below[0] = jnp.zeros((rows_c, height), jnp.float32)

    @pl.when(has_prev & jnp.logical_not(has_high))
    def _():
        below[1] = jnp.zeros((rows_c, height), jnp.float32)

    body_hop = time_hop(3, ahead, delta)
    up_hop = time_hop(4, ahead.at[depth_c - 1], below.at[0], 1)
    down_hop = time_hop(5, ahead.at[0], below.at[1], -1)
    start_hop.wait_recv()

    def combine_start(z, r, chunk):
        at = pl.ds(r, chunk)
        total = (slice_length * float(INTEGRALS[0, 0])) * start[z, at]
        for node in range(1, NODES):
            total = total + (slice_length * float(INTEGRALS[0, node])) * fields[node, z, at]
        fill(2, z, r, total)

    pl.when(has_prev)(lambda: edges(combine_start))
    lift_hop.wait_recv()
    gain[...] = gain[...] + moved[...]
    body_hop.wait_recv()
    up_hop.wait_recv()
    down_hop.wait_recv()
    for zc in range(depth_c):
        center = delta[zc]
        under = below[0] if zc == 0 else delta[zc - 1]
        over = below[1] if zc == depth_c - 1 else delta[zc + 1]
        behind = pltpu.roll(center, 1, 0)
        across = behind + pltpu.roll(center, rows_c - 1, 0)
        lateral = sideways(center)
        spreading = kappa_c[zc] * (
            (under + over - 2.0 * center) * (1.0 / (BLOCK_Z * BLOCK_Z))
            + (across - 2.0 * center) * (1.0 / (BLOCK_X * BLOCK_X))
            + (lateral - 2.0 * center)
        )
        flow = (1.0 / BLOCK_X) * advect * (center - behind)
        ahead[zc] = center + slice_length * (spreading - flow) + gain[zc]
        if zc == 0:
            send(down_hop)
        if zc == depth_c - 1:
            send(up_hop)
    send(body_hop)

    for zc in range(depth_c):
        for k in range(BLOCK_X):
            spread[0, zc, pl.ds(k, rows_c, stride=BLOCK_X)] = delta[zc]
            spread[1, zc, pl.ds(k, rows_c, stride=BLOCK_X)] = ahead[zc]

    @pl.when(jnp.logical_not(has_prev))
    def _():
        def turn(z, carry):
            start[z] = fields[0, z]
            return carry

        lax.fori_loop(0, depth, turn, 0)
        edges(combine_start)

    late = slice_length * float((INTEGRALS[0] * TIMES).sum())
    early = slice_length * float(INTEGRALS[0].sum()) - late

    def correct_edge(z, r, chunk):
        at, zc = pl.ds(r, chunk), z // BLOCK_Z
        base = pads[2, z + 1, pl.ds(PAD + r, chunk)]
        fill(2, z, r, base + (early * spread[0, zc, at] + late * spread[1, zc, at]))

    def correct(z, r, chunk):
        at = pl.ds(r, chunk)
        zc = z // BLOCK_Z
        begin, ending = spread[0, zc, at], spread[1, zc, at]
        total = None
        for node in range(NODES):
            weight = float(TIMES[node])
            own = start[z, at] if node == 0 else fields[node, z, at]
            if node == 0:
                value = own + begin
                out[0, z, at] = value
            elif node == last:
                value = own + ending
            else:
                value = own + ((1.0 - weight) * begin + weight * ending)
            if node > 0:
                values[node - 1, z, at] = value
            term = (slice_length * float(INTEGRALS[0, node])) * value
            total = term if total is None else total + term
        if not isinstance(z, int):
            fill(2, z, r, total)

    pair = halo(2)
    edges(correct_edge, None, pair)
    edges(correct)
    interior(correct)

    for sweep in range(FINE_SWEEPS):
        old = values if sweep == 0 else mids
        new = mids if sweep == 0 else None
        for step in range(STEPS):
            index = 2 + sweep * STEPS + step
            final = sweep == FINE_SWEEPS - 1
            more = not (final and step == STEPS - 1)

            def advance(z, r, chunk, index=index, step=step, old=old, new=new, final=final, more=more):
                at = pl.ds(r, chunk)
                if step == 0:
                    before = out[0, z, at]
                else:
                    before = out[step, z, at] if final else new[step - 1, z, at]
                value = before + rate(index, z, r, advect, chunk)
                if final:
                    out[step + 1, z, at] = value
                else:
                    new[step, z, at] = value
                if not more:
                    return
                if step < STEPS - 1:
                    gap = slice_length * float(TIMES[step + 2] - TIMES[step + 1])
                    total = gap * (value - old[step, z, at])
                    row, source, known = step + 1, old, {}
                else:
                    total, row, source, known = None, 0, new, {STEPS: value}
                for node in range(NODES):
                    if node == 0:
                        part = out[0, z, at]
                    else:
                        part = known[node] if node in known else source[node - 1, z, at]
                    term = (slice_length * float(INTEGRALS[row, node])) * part
                    total = term if total is None else total + term
                fill(index + 1, z, r, total)

            following = halo(index + 1) if more else None
            edges(advance, pair, following)
            interior(advance)
            pair = following

    groups = {}
    for transfer in shipped:
        groups.setdefault(id(transfer.sends), []).append(transfer)
    for group in groups.values():

        @pl.when(group[0].sends)
        def _(group=group):
            for transfer in group:
                transfer.copy.wait_send()


def shards(node_fields, region_label, sheet_shift, diffusivity):
    fields = node_fields[0]
    nodes, depth, width, height = fields.shape
    depth_c, rows_c = depth // BLOCK_Z, width // BLOCK_X
    f32 = jnp.float32
    fine = (depth, width, height)
    coarse = (depth_c, rows_c, height)
    vmem, hbm = (pl.BlockSpec(memory_space=space) for space in (pltpu.VMEM, pltpu.HBM))
    result = pl.pallas_call(
        kernel,
        out_shape=jax.ShapeDtypeStruct(fields.shape, f32),
        in_specs=[hbm] * 4,
        out_specs=vmem,
        scratch_shapes=[
            pltpu.VMEM(fields.shape, f32),
            pltpu.VMEM(fine, jnp.int32),
            pltpu.VMEM(sheet_shift.shape, jnp.int32),
            pltpu.SMEM(diffusivity.shape, f32),
            pltpu.VMEM(fine, f32),
            pltpu.VMEM(coarse, f32),
            pltpu.VMEM(fine, f32),
            pltpu.VMEM(coarse, f32),
            pltpu.VMEM(sheet_shift.shape, jnp.int32),
            pltpu.VMEM((2, rows_c, height), f32),
            pltpu.VMEM((EXCHANGES, depth + 2, width + 2 * PAD, height), f32),
            pltpu.VMEM((STEPS,) + fine, f32),
            pltpu.VMEM((STEPS,) + fine, f32),
            pltpu.VMEM((2, depth_c, width, height), f32),
            pltpu.VMEM(coarse, f32),
            pltpu.VMEM(coarse, f32),
            pltpu.VMEM(coarse, f32),
            pltpu.VMEM(coarse, f32),
            pltpu.VMEM((width, height), f32),
            pltpu.SemaphoreType.DMA((2 * EXCHANGES * PIECES,)),
            pltpu.SemaphoreType.DMA((2 * EXCHANGES * PIECES,)),
            pltpu.SemaphoreType.DMA((6,)),
            pltpu.SemaphoreType.DMA((6,)),
            pltpu.SemaphoreType.DMA((NODES + 3,)),
        ],
        compiler_params=pltpu.CompilerParams(
            collective_id=0, has_side_effects=True, vmem_limit_bytes=48 * 1024 * 1024
        ),
    )(*(pltpu.with_memory_space_constraint(x, pltpu.HBM) for x in (fields, region_label, sheet_shift, diffusivity)))
    return result[None]


def solution(mesh):
    in_specs = (P("tm", None, "space", None, None), P("space", None, None), P("tm", None), P())
    out_specs = P("tm", None, "space", None, None)
    return jax.shard_map(shards, mesh=mesh, in_specs=in_specs, out_specs=out_specs, check_vma=False)
```

profile of v0, /device:TPU:6, one launch (start us, length us, event | category | flops | bytes accessed | tf_op | source)
XLA Modules:
  0.0 55.7 jit_solution(14022481530276309879)
XLA Ops:
  0.0 54.2 %shard_map.46 = f32[5,8,128,128]{3,2,1,0:T(8,128)S(1)} custom-call(f32[5,8,128,128]{3,2,1,0:T(8,128)} %bitcast.3, s32[8,128,128]{2,1,0:T(8,128)} %label_in.1, s32[1,128]{1,0:T(1,128)} %shift_in.1, f32[4]{0:T(128)} %table_in.1), custom_call_target="tpu_custom_call" | custom-call | tf_op jit(solution)/shard_map/pallas_call | solution.py:449
  54.2 1.5 %copy.6 = f32[1,5,8,128,128]{4,3,2,1,0:T(8,128)} copy(f32[1,5,8,128,128]{4,3,2,1,0:T(8,128)S(1)} %bitcast.2) | data formatting | bytes 5242880
where the time goes:
time: 55.9 us; the launch traced here: 55.7 us
  Pallas kernels  54.2 us (97%)
  local copies, waits for them, and re-layouts  1.49 us (3%)
    pallas_call x1, Pallas kernels, shards(): pl.pallas_call(kernel, out_shape=jax.ShapeDtypeStruct(fields.shape, f32),...  54.2 us
    unnamed x1, local copies, waits for them, and re-layouts  1.49 us

commit v1 on v0

v1 whole, which is shorter than its diff:
```python
import math

import jax
import jax.numpy as jnp
import numpy as np
from jax import lax
from jax.experimental import pallas as pl
from jax.experimental.pallas import tpu as pltpu
from jax.sharding import PartitionSpec as P

NODES = 5
FINE_SWEEPS = 2
BLOCK_Z = 4
BLOCK_X = 2
PAD = 8
PIECES = 4
MESH = pl.DeviceIdType.MESH

slice_length = 1.0


def node_tables():
    radius = math.sqrt(3.0 / 7.0)
    points = [0.0, (1.0 - radius) / 2.0, 0.5, (1.0 + radius) / 2.0, 1.0]
    integrals = np.zeros((4, 5))
    for column in range(5):
        coeffs = [1.0]
        divisor = 1.0
        for other in range(5):
            if other != column:
                anchor = points[other]
                product = [0.0] * (len(coeffs) + 1)
                for degree in range(len(coeffs)):
                    product[degree + 1] = product[degree + 1] + coeffs[degree]
                    product[degree] = product[degree] - anchor * coeffs[degree]
                coeffs = product
                divisor = divisor * (points[column] - anchor)
        for row in range(4):
            bottom = points[row]
            summit = points[row + 1]
            amount = 0.0
            for degree in range(len(coeffs)):
                amount = amount + coeffs[degree] / (degree + 1) * (
                    summit ** (degree + 1) - bottom ** (degree + 1)
                )
            integrals[row, column] = amount / divisor
    return (np.array(points), integrals)


TIMES, INTEGRALS = node_tables()
WEIGHTS = INTEGRALS.sum(axis=0)
STEPS = NODES - 1
REACH = FINE_SWEEPS * STEPS
EXCHANGES = 3 + REACH
FIRST = EXCHANGES - 1
GAPS = TIMES[1:] - TIMES[:-1]
LATE = (INTEGRALS * TIMES).sum(axis=1)
EARLY = INTEGRALS.sum(axis=1) - LATE
CHAIN_SLOTS = REACH - 1


class Transfer:
    def __init__(self, src, dst, send_sem, recv_sem, device, sends, receives):
        self.copy = pltpu.make_async_remote_copy(
            src_ref=src,
            dst_ref=dst,
            send_sem=send_sem,
            recv_sem=recv_sem,
            device_id=device,
            device_id_type=MESH,
        )
        self.sends, self.receives = sends, receives

    def start(self):
        pl.when(self.sends)(self.copy.start)

    def wait_recv(self):
        pl.when(self.receives)(self.copy.wait_recv)

    def wait_send(self):
        pl.when(self.sends)(self.copy.wait_send)


def kernel(
    fields_in, label_in, shift_in, table_in, out, fields, label, shift, table,
    kappa, kappa_c, start, rim, moved, shift_next, below, pads, mids, gain, lift, delta, fold,
    spread, base, grid, nodes, latest,
    halo_send, halo_recv, time_send, time_recv, wide_send, wide_recv, label_send, label_recv, load_sem,
):
    n, s = lax.axis_index("tm"), lax.axis_index("space")
    slices, slabs = lax.axis_size("tm"), lax.axis_size("space")
    depth, width, height = fields.shape[1:]
    rows_c = width // BLOCK_X
    depth_c = depth // BLOCK_Z
    near = -(-REACH // depth)
    own, own_c = near * depth, near * depth_c
    layers, layers_c = (2 * near + 1) * depth, (2 * near + 1) * depth_c
    chunk = min(64, width)
    piece = width // PIECES
    last = NODES - 1
    has_prev, has_next = n > 0, n < slices - 1
    has_low, has_high = s > 0, s < slabs - 1
    inner = pl.ds(PAD, width)
    here_c = pl.ds(own_c, depth_c)

    loads = [
        pltpu.make_async_copy(fields_in.at[node], fields.at[node], load_sem.at[node])
        for node in range(NODES)
    ]
    loads += [
        pltpu.make_async_copy(label_in, label.at[pl.ds(own, depth)], load_sem.at[NODES]),
        pltpu.make_async_copy(shift_in, shift, load_sem.at[NODES + 1]),
        pltpu.make_async_copy(table_in, table, load_sem.at[NODES + 2]),
    ]
    for load in loads:
        load.start()

    barrier = pltpu.get_barrier_semaphore()
    met = jnp.int32(0)
    for dn in (-1, 0, 1):
        span = near if dn == 0 else 1
        for ds in range(-span, span + 1):
            if dn == 0 and ds == 0:
                continue
            there = (n + dn >= 0) & (n + dn < slices) & (s + ds >= 0) & (s + ds < slabs)

            @pl.when(there)
            def _(dn=dn, ds=ds):
                pl.semaphore_signal(
                    barrier, inc=1, device_id={"tm": n + dn, "space": s + ds}, device_id_type=MESH
                )

            met = met + there.astype(jnp.int32)
    pl.semaphore_wait(barrier, met)

    shipped = []

    def send(transfer):
        transfer.start()
        shipped.append(transfer)
        return transfer

    def halo(index, source=None):
        buf = pads.at[index]
        pieces = []
        for k in range(PIECES):
            rows = pl.ds(PAD + k * piece, piece)
            if source is None:
                low, high = buf.at[1, rows], buf.at[depth, rows]
            else:
                low, high = (source.at[z, pl.ds(k * piece, piece)] for z in (0, depth - 1))
            sem = 2 * (index * PIECES + k)
            up = Transfer(
                high, buf.at[0, rows], halo_send.at[sem], halo_recv.at[sem],
                {"space": s + 1}, has_high, has_low,
            )
            down = Transfer(
                low, buf.at[depth + 1, rows], halo_send.at[sem + 1], halo_recv.at[sem + 1],
                {"space": s - 1}, has_low, has_high,
            )
            pieces.append((down, up))
        return pieces

    def arrive(pieces):
        for down, up in pieces:
            down.wait_recv()
            up.wait_recv()

    def time_hop(index, src, dst, ds=0):
        to = {"tm": n + 1} if ds == 0 else {"tm": n + 1, "space": s + ds}
        goes = has_next if ds == 0 else has_next & (s + ds >= 0) & (s + ds < slabs)
        comes = has_prev if ds == 0 else has_prev & (s - ds >= 0) & (s - ds < slabs)
        return Transfer(src, dst, time_send.at[index], time_recv.at[index], to, goes, comes)

    within = {
        distance: (s + distance >= 0) & (s + distance < slabs)
        for distance in range(-near, near + 1)
    }

    shift_hop = Transfer(
        shift_in, shift_next, time_send.at[0], time_recv.at[0], {"tm": n - 1}, has_prev, has_next
    )
    send(shift_hop)
    end_halo = halo(1, fields_in.at[last])
    for down, up in end_halo:
        send(down)
        send(up)
    rim_hops = [
        send(time_hop(6, fields_in.at[last, depth - 1], rim.at[0], 1)),
        send(time_hop(7, fields_in.at[last, 0], rim.at[1], -1)),
    ]
    start_hop = send(time_hop(1, fields_in.at[last], start))

    label_hops = []
    for distance in range(1, near + 1):
        for z in range(depth):
            for sign in (1, -1):
                there = own - sign * distance * depth + z
                sem = 2 * ((distance - 1) * depth + z) + (sign + 1) // 2
                label_hops.append(
                    Transfer(
                        label_in.at[z], label.at[there], label_send.at[sem], label_recv.at[sem],
                        {"space": s + sign * distance}, within[sign * distance], within[-sign * distance],
                    )
                )
    label_queue = list(label_hops)

    def send_labels(count):
        for transfer in label_queue[:count]:
            send(transfer)
        del label_queue[:count]

    wide_hops = []
    for field in range(2):
        for distance in range(1, near + 1):
            for sign in (1, -1):
                there = pl.ds(own_c - sign * distance * depth_c, depth_c)
                sem = 2 * (field * near + distance - 1) + (sign + 1) // 2
                wide_hops.append(
                    Transfer(
                        delta.at[field, here_c], delta.at[field, there], wide_send.at[sem], wide_recv.at[sem],
                        {"space": s + sign * distance}, within[sign * distance], within[-sign * distance],
                    )
                )

    first_slice = (n == 0).astype(jnp.float32)

    def sideways(center):
        lane = lax.broadcasted_iota(jnp.int32, center.shape, 1)
        return jnp.where(lane == height - 1, 0.0, pltpu.roll(center, height - 1, 1)) + jnp.where(
            lane == 0, 0.0, pltpu.roll(center, 1, 1)
        )

    def slope(buf, layer, r, advect, weight, rows):
        center = buf[layer, pl.ds(PAD + r, rows)]
        behind = buf[layer, pl.ds(PAD - 1 + r, rows)]
        total = buf[layer - 1, pl.ds(PAD + r, rows)] + buf[layer + 1, pl.ds(PAD + r, rows)]
        total = total + (behind + buf[layer, pl.ds(PAD + 1 + r, rows)])
        total = total + sideways(center) - 6.0 * center
        return weight * total - advect * (center - behind)

    def rate(index, z, r, advect, chunk=chunk):
        return slope(pads.at[index], z + 1, r, advect, kappa[own + z, pl.ds(r, chunk)], chunk)

    def place(buf, layer, r, value):
        rows = value.shape[0]
        buf[layer, pl.ds(PAD + r, rows)] = value
        if r == 0:
            buf[layer, pl.ds(PAD + width, 1)] = value[:1]
        if r + rows == width:
            buf[layer, pl.ds(PAD - 1, 1)] = value[rows - 1 :]

    def fill(index, z, r, value):
        place(pads.at[index], z + 1, r, value)

    def each(lo, hi, body):
        def turn(z, carry):
            for r in range(0, width, chunk):
                body(z, r, chunk)
            return carry

        lax.fori_loop(lo, hi, turn, 0)

    def edges(body, needs=None, gives=None):
        for k in range(PIECES):
            if needs is not None:
                arrive(needs[k : k + 1])
            body(0, k * piece, piece)
            body(depth - 1, k * piece, piece)
            if gives is not None:
                send(gives[k][0])
                send(gives[k][1])

    def interior(body):
        each(1, depth - 1, body)

    def combine(coefficients, first, z, r, chunk):
        at = pl.ds(r, chunk)
        total = (first_slice * float(coefficients[0])) * fields[0, z, at] if first is None else first
        for node in range(1, NODES):
            total = total + float(coefficients[node]) * fields[node, z, at]
        return total

    def weigh(z, r, chunk):
        fill(0, z, r, combine(slice_length * WEIGHTS, None, z, r, chunk))

    def foresee(z, r, chunk):
        fill(FIRST, z, r, combine(slice_length * INTEGRALS[0], None, z, r, chunk))

    for load in loads:
        load.wait()
    weighted_halo = halo(0)
    edges(weigh, None, weighted_halo)
    first_halo = halo(FIRST)
    edges(foresee, None, first_halo)
    interior(weigh)

    def look_up(layer, r, chunk):
        at = pl.ds(r, chunk)
        labels = label[layer, at]
        total = jnp.zeros((chunk, height), jnp.float32)
        for region in range(table.shape[0]):
            total = total + jnp.where(labels == region, table[region], 0.0)
        kappa[layer, at] = total

    def prepare(z, r, chunk):
        fill(1, z, r, fields[last, z, pl.ds(r, chunk)])
        look_up(own + z, r, chunk)

    each(0, depth, prepare)

    for index in range(EXCHANGES):

        @pl.when(jnp.logical_not(has_low))
        def _(index=index):
            pads[index, 0, inner] = jnp.zeros((width, height), jnp.float32)

        @pl.when(jnp.logical_not(has_high))
        def _(index=index):
            pads[index, depth + 1, inner] = jnp.zeros((width, height), jnp.float32)

    def restrict(target, layer_of):
        def turn(zc, carry):
            for r in range(0, width, chunk):
                total = layer_of(BLOCK_Z * zc, r)
                for k in range(1, BLOCK_Z):
                    total = total + layer_of(BLOCK_Z * zc + k, r)
                fold[pl.ds(r, chunk)] = total
            total = fold[pl.ds(0, rows_c, stride=BLOCK_X)]
            for k in range(1, BLOCK_X):
                total = total + fold[pl.ds(k, rows_c, stride=BLOCK_X)]
            target[zc] = total * (1.0 / (BLOCK_Z * BLOCK_X))
            return carry

        lax.fori_loop(0, depth_c, turn, 0)

    advect = shift[...].astype(jnp.float32) / slice_length

    arrive(weighted_halo)
    restrict(
        gain,
        lambda z, r: first_slice * fields[0, z, pl.ds(r, chunk)]
        - fields[last, z, pl.ds(r, chunk)]
        + slice_length * rate(0, z, r, advect),
    )
    restrict(kappa_c, lambda z, r: kappa[own + z, pl.ds(r, chunk)])

    @pl.when(jnp.logical_not(has_prev))
    def _():
        moved[...] = jnp.zeros_like(moved)
        delta[0, here_c] = jnp.zeros((depth_c, rows_c, height), jnp.float32)
        below[...] = jnp.zeros_like(below)

    @pl.when(has_prev & jnp.logical_not(has_low))
    def _():
        below[0] = jnp.zeros((rows_c, height), jnp.float32)

    @pl.when(has_prev & jnp.logical_not(has_high))
    def _():
        below[1] = jnp.zeros((rows_c, height), jnp.float32)

    for distance in range(1, near + 1):
        for sign in (1, -1):

            @pl.when(jnp.logical_not(within[sign * distance]))
            def _(distance=distance, sign=sign):
                there = own_c + sign * distance * depth_c
                delta[:, pl.ds(there, depth_c)] = jnp.zeros((2, depth_c, rows_c, height), jnp.float32)

    lift_hop = time_hop(2, lift, moved)
    body_hop = time_hop(3, delta.at[1, here_c], delta.at[0, here_c])
    up_hop = time_hop(4, delta.at[1, own_c + depth_c - 1], below.at[0], 1)
    down_hop = time_hop(5, delta.at[1, own_c], below.at[1], -1)
    shipped.extend([body_hop, up_hop, down_hop] + wide_hops)

    def chain():
        lift_hop.wait_recv()
        body_hop.wait_recv()
        up_hop.wait_recv()
        down_hop.wait_recv()
        for zc in range(depth_c):
            center = delta[0, own_c + zc]
            under = below[0] if zc == 0 else delta[0, own_c + zc - 1]
            over = below[1] if zc == depth_c - 1 else delta[0, own_c + zc + 1]
            behind = pltpu.roll(center, 1, 0)
            across = behind + pltpu.roll(center, rows_c - 1, 0)
            lateral = sideways(center)
            spreading = kappa_c[zc] * (
                (under + over - 2.0 * center) * (1.0 / (BLOCK_Z * BLOCK_Z))
                + (across - 2.0 * center) * (1.0 / (BLOCK_X * BLOCK_X))
                + (lateral - 2.0 * center)
            )
            flow = (1.0 / BLOCK_X) * advect * (center - behind)
            delta[1, own_c + zc] = center + slice_length * (spreading - flow) + (gain[zc] + moved[zc])
            if zc == 0:
                down_hop.start()
            if zc == depth_c - 1:
                up_hop.start()
        body_hop.start()
        for transfer in wide_hops:
            transfer.start()

    pl.when(n == 0)(chain)

    shift_hop.wait_recv()
    arrive(end_halo)
    advect_next = shift_next[...].astype(jnp.float32) / slice_length
    restrict(
        lift,
        lambda z, r: fields[last, z, pl.ds(r, chunk)]
        + (slice_length * float(WEIGHTS[0])) * rate(1, z, r, advect_next),
    )
    send(lift_hop)

    @pl.when(jnp.logical_not(has_prev))
    def _():
        def turn(z, carry):
            start[z] = fields[0, z]
            return carry

        lax.fori_loop(0, depth, turn, 0)
        rim[...] = jnp.zeros_like(rim)

    for end, there in enumerate((has_low, has_high)):

        @pl.when(has_prev & jnp.logical_not(there))
        def _(end=end):
            rim[end] = jnp.zeros((width, height), jnp.float32)

    start_hop.wait_recv()
    rim_hops[0].wait_recv()
    rim_hops[1].wait_recv()
    begin_weight = slice_length * float(INTEGRALS[0, 0])

    def combine_start(z, r, chunk):
        fill(2, z, r, combine(slice_length * INTEGRALS[0], begin_weight * start[z, pl.ds(r, chunk)], z, r, chunk))

    each(0, depth, combine_start)
    arrive(first_halo)
    for end, layer in ((0, 0), (1, depth + 1)):
        for r in range(0, width, chunk):
            at = pl.ds(PAD + r, chunk)
            pads[2, layer, at] = pads[FIRST, layer, at] + begin_weight * rim[end, pl.ds(r, chunk)]

    def fine_step(sweep, step, needs):
        old = fields if sweep == 0 else mids
        new = mids if sweep == 0 else None
        offset = 0 if sweep == 0 else -1
        index = 2 + sweep * STEPS + step
        final = sweep == FINE_SWEEPS - 1
        more = not (final and step == STEPS - 1)

        def advance(z, r, chunk):
            at = pl.ds(r, chunk)
            if step == 0:
                before = start[z, at]
            else:
                before = out[step, z, at] if final else new[step - 1, z, at]
            value = before + rate(index, z, r, advect, chunk)
            if final:
                out[step + 1, z, at] = value
            else:
                new[step, z, at] = value
            if not more:
                return
            if step < STEPS - 1:
                total = slice_length * float(GAPS[step + 1]) * (value - old[step + 1 + offset, z, at])
                row, source, shown, known = step + 1, old, offset, {}
            else:
                total, row, source, shown, known = None, 0, new, -1, {STEPS: value}
            for node in range(NODES):
                if node == 0:
                    part = start[z, at]
                else:
                    part = known[node] if node in known else source[node + shown, z, at]
                term = (slice_length * float(INTEGRALS[row, node])) * part
                total = term if total is None else total + term
            fill(index + 1, z, r, total)

        following = halo(index + 1) if more else None
        edges(advance, needs, following)
        return following, lambda: interior(advance)

    pair = None
    quota = -(-len(label_hops) // (2 * STEPS - 4))
    for stage in range(REACH - 2):
        if stage > 0:
            waiting = (n == stage) if stage < CHAIN_SLOTS else (n >= stage)
            pl.when(waiting)(chain)
        pair, rest = fine_step(stage // STEPS, stage % STEPS, pair)
        send_labels(quota)
        rest()

    for transfer in label_hops:
        transfer.wait_recv()
    for distance in range(1, near + 1):
        for sign in (1, -1):
            low = own + sign * distance * depth
            there = within[sign * distance]

            @pl.when(there)
            def _(low=low):
                each(low, low + depth, look_up)

            @pl.when(jnp.logical_not(there))
            def _(low=low):
                def turn(z, carry):
                    kappa[z] = jnp.zeros((width, height), jnp.float32)
                    return carry

                lax.fori_loop(low, low + depth, turn, 0)

    pl.when(n >= REACH - 2)(chain)
    pair, rest = fine_step(FINE_SWEEPS - 1, STEPS - 2, pair)
    rest()

    for transfer in wide_hops:
        transfer.wait_recv()

    def widen(c, carry):
        for field in range(2):
            for k in range(BLOCK_X):
                spread[field, c, pl.ds(k, rows_c, stride=BLOCK_X)] = delta[field, c]
        for r in range(0, width, chunk):
            at = pl.ds(r, chunk)
            place(base, c + 1, r, mix(EARLY[0], LATE[0], c, at))
        return carry

    def mix(early, late, c, at):
        return (slice_length * float(early)) * spread[0, c, at] + (slice_length * float(late)) * spread[1, c, at]

    lax.fori_loop(0, layers_c, widen, 0)
    base[0, inner] = jnp.zeros((width, height), jnp.float32)
    base[layers_c + 1, inner] = jnp.zeros((width, height), jnp.float32)

    def later(row, c, at):
        gap = float(GAPS[row])
        weight = float(TIMES[row])
        return mix(EARLY[row] - gap * (1.0 - weight), LATE[row] - gap * weight, c, at)

    def open_step(c, carry):
        for r in range(0, width, chunk):
            at, inside = pl.ds(r, chunk), pl.ds(PAD + r, chunk)
            center = base[c + 1, inside]
            behind = base[c + 1, pl.ds(PAD - 1 + r, chunk)]
            level = behind + base[c + 1, pl.ds(PAD + 1 + r, chunk)] + sideways(center)
            flow = advect * (center - behind)
            initial, following = spread[0, c, at], later(1, c, at)
            for k in range(BLOCK_Z):
                layer = BLOCK_Z * c + k
                total = level - (4.0 if 0 < k < BLOCK_Z - 1 else 5.0) * center
                if k == 0:
                    total = total + base[c, inside]
                if k == BLOCK_Z - 1:
                    total = total + base[c + 2, inside]
                value = initial + (kappa[layer, at] * total - flow)
                nodes[0, layer, at] = value
                place(grid.at[0], layer, r, float(GAPS[1]) * slice_length * value + following)
        return carry

    def wide_each(margin, body):
        def outer(i, carry):
            layer = own - margin + i + jnp.where(i >= margin, depth, 0)
            for r in range(0, width, chunk):
                body(layer, None, r)
            return carry

        def middle(z, carry):
            for r in range(0, width, chunk):
                body(own + z, z, r)
            return carry

        if margin > 0:
            lax.fori_loop(0, 2 * margin, outer, 0)
        lax.fori_loop(0, depth, middle, 0)

    def wide_step(stage):
        sweep, step = stage // STEPS, stage % STEPS
        source, target = grid.at[(stage - 1) % 2], grid.at[stage % 2]
        margin = REACH - 1 - stage
        final = sweep == FINE_SWEEPS - 1
        more = stage < REACH - 1

        def advance(layer, z, r):
            at, c = pl.ds(r, chunk), layer // BLOCK_Z
            initial = spread[0, c, at]
            if step == 0:
                before = initial
            else:
                before = latest[layer, at] if final else nodes[step - 1, layer, at]
            value = before + slope(source, layer, r, advect, kappa[layer, at], chunk)
            if final:
                if more:
                    latest[layer, at] = value
                if z is not None:
                    out[step + 1, z, at] = out[step + 1, z, at] + value
                    if step == 0:
                        out[0, z, at] = start[z, at] + initial
            else:
                nodes[step, layer, at] = value
            if not more:
                return
            if not final and step < STEPS - 1:
                total = slice_length * float(GAPS[step + 1]) * value + later(step + 1, c, at)
            else:
                if final:
                    row, known = step + 1, {}
                    total = slice_length * float(GAPS[row]) * (value - nodes[step, layer, at])
                else:
                    row, known = 0, {STEPS: value}
                    total = 0.0
                total = total + (slice_length * float(INTEGRALS[row, 0])) * initial
                for node in range(1, NODES):
                    part = known[node] if node in known else nodes[node - 1, layer, at]
                    total = total + (slice_length * float(INTEGRALS[row, node])) * part
            place(target, layer, r, total)

        wide_each(margin, advance)

    lax.fori_loop(0, layers_c, open_step, 0)
    for stage in range(1, STEPS):
        wide_step(stage)
    pair, rest = fine_step(FINE_SWEEPS - 1, STEPS - 1, pair)
    rest()
    for stage in range(STEPS, REACH):
        wide_step(stage)

    groups = {}
    for transfer in shipped:
        groups.setdefault(id(transfer.sends), []).append(transfer)
    for group in groups.values():

        @pl.when(group[0].sends)
        def _(group=group):
            for transfer in group:
                transfer.copy.wait_send()


def shards(node_fields, region_label, sheet_shift, diffusivity):
    fields = node_fields[0]
    nodes, depth, width, height = fields.shape
    depth_c, rows_c = depth // BLOCK_Z, width // BLOCK_X
    near = -(-REACH // depth)
    layers, layers_c = (2 * near + 1) * depth, (2 * near + 1) * depth_c
    f32 = jnp.float32
    fine, wide = (depth, width, height), (layers, width, height)
    coarse = (depth_c, rows_c, height)
    padded = width + 2 * PAD
    vmem, hbm = (pl.BlockSpec(memory_space=space) for space in (pltpu.VMEM, pltpu.HBM))
    result = pl.pallas_call(
        kernel,
        out_shape=jax.ShapeDtypeStruct(fields.shape, f32),
        in_specs=[hbm] * 4,
        out_specs=vmem,
        scratch_shapes=[
            pltpu.VMEM(fields.shape, f32),
            pltpu.VMEM(wide, jnp.int32),
            pltpu.VMEM(sheet_shift.shape, jnp.int32),
            pltpu.SMEM(diffusivity.shape, f32),
            pltpu.VMEM(wide, f32),
            pltpu.VMEM(coarse, f32),
            pltpu.VMEM(fine, f32),
            pltpu.VMEM((2, width, height), f32),
            pltpu.VMEM(coarse, f32),
            pltpu.VMEM(sheet_shift.shape, jnp.int32),
            pltpu.VMEM((2, rows_c, height), f32),
            pltpu.VMEM((EXCHANGES, depth + 2, padded, height), f32),
            pltpu.VMEM((STEPS,) + fine, f32),
            pltpu.VMEM(coarse, f32),
            pltpu.VMEM(coarse, f32),
            pltpu.VMEM((2, layers_c, rows_c, height), f32),
            pltpu.VMEM((width, height), f32),
            pltpu.VMEM((2, layers_c, width, height), f32),
            pltpu.VMEM((layers_c + 2, padded, height), f32),
            pltpu.VMEM((2, layers, padded, height), f32),
            pltpu.VMEM((STEPS,) + wide, f32),
            pltpu.VMEM(wide, f32),
            pltpu.SemaphoreType.DMA((2 * EXCHANGES * PIECES,)),
            pltpu.SemaphoreType.DMA((2 * EXCHANGES * PIECES,)),
            pltpu.SemaphoreType.DMA((8,)),
            pltpu.SemaphoreType.DMA((8,)),
            pltpu.SemaphoreType.DMA((4 * near,)),
            pltpu.SemaphoreType.DMA((4 * near,)),
            pltpu.SemaphoreType.DMA((2 * near * depth,)),
            pltpu.SemaphoreType.DMA((2 * near * depth,)),
            pltpu.SemaphoreType.DMA((NODES + 3,)),
        ],
        compiler_params=pltpu.CompilerParams(
            collective_id=0, has_side_effects=True, vmem_limit_bytes=48 * 1024 * 1024
        ),
    )(*(pltpu.with_memory_space_constraint(x, pltpu.HBM) for x in (fields, region_label, sheet_shift, diffusivity)))
    return result[None]


def solution(mesh):
    in_specs = (P("tm", None, "space", None, None), P("space", None, None), P("tm", None), P())
    out_specs = P("tm", None, "space", None, None)
    return jax.shard_map(shards, mesh=mesh, in_specs=in_specs, out_specs=out_specs, check_vma=False)
```

time: 55.9 us -> 59.2 us (1.059)
  the two profiles are of different devices: /device:TPU:6 before, /device:TPU:7 now
where the time goes in v1:
time: 59.2 us; the launch traced here: 59 us
  Pallas kernels  57.5 us (97%)
  local copies, waits for them, and re-layouts  1.49 us (3%)
    pallas_call x1, Pallas kernels, shards(): pl.pallas_call(kernel, out_shape=jax.ShapeDtypeStruct(fields.shape, f32),...  57.5 us
    unnamed x1, local copies, waits for them, and re-layouts  1.49 us

profile of v1, /device:TPU:7, one launch (start us, length us, event | category | flops | bytes accessed | tf_op | source)
XLA Modules:
  0.0 59.0 jit_solution(5777296619423161511)
XLA Ops:
  0.0 57.5 %shard_map.46 = f32[5,8,128,128]{3,2,1,0:T(8,128)S(1)} custom-call(f32[5,8,128,128]{3,2,1,0:T(8,128)} %bitcast.3, s32[8,128,128]{2,1,0:T(8,128)} %label_in.1, s32[1,128]{1,0:T(1,128)} %shift_in.1, f32[4]{0:T(128)} %table_in.1), custom_call_target="tpu_custom_call" | custom-call | tf_op jit(solution)/shard_map/pallas_call | solution.py:650
  57.5 1.5 %copy.6 = f32[1,5,8,128,128]{4,3,2,1,0:T(8,128)} copy(f32[1,5,8,128,128]{4,3,2,1,0:T(8,128)S(1)} %bitcast.2) | data formatting | bytes 5242880
